TPU v7x, 32 devices: a whole 2x2x4 slice. The times are simulated.
32 devices in a mesh: dp: 4 (over z), expert: 4 (over y, x), seq: 2 (over core).
Axes of the slice: x: 2, y: 2, z: 4, core: 2. Of those that a mesh axis runs over, the one named last changes fastest.
Arguments:
- tokens: bfloat16 [4096, 2048], P(('dp', 'expert', 'seq')), may hold values from -6 to 6
- out_grad: bfloat16 [4096, 2048], P(('dp', 'expert', 'seq')), may hold values from -6 to 6
- expert_ids: int32 [4096, 2], P(('dp', 'expert', 'seq')), may hold values from 0 to 3, all different within a row; in each aligned block of 128 rows (0 to 127, 128 to 255, ...) at most 96 rows name the same one
- gate_values: float32 [4096, 2], P(('dp', 'expert', 'seq')), may hold values from 0.2 to 1
- gate_weight: bfloat16 [4, 2048, 512], P('expert', 'dp', 'seq'), may hold values from -0.125 to 0.125
- up_weight: bfloat16 [4, 2048, 512], P('expert', 'dp', 'seq'), may hold values from -0.125 to 0.125
- down_weight: bfloat16 [4, 2048, 512], P('expert', 'dp', 'seq'), may hold values from -0.25 to 0.25
Outputs:
- in_grad: bfloat16 [4096, 2048], P(('dp', 'expert', 'seq'))
- gate_grads: float32 [4096, 2], P(('dp', 'expert', 'seq'))
- gate_weight_grad: bfloat16 [4, 2048, 512], P('expert', 'dp', 'seq')
- up_weight_grad: bfloat16 [4, 2048, 512], P('expert', 'dp', 'seq')
- down_weight_grad: bfloat16 [4, 2048, 512], P('expert', 'dp', 'seq')
Inputs may be any that keep to these rules, and one draw needn't show every extreme that they name: `expert_ids`: the two ids of a row differ. Within the 128 rows of one device no expert is named more than 96 times, a bound that some block reaches.
All inputs are finite; a program needn't handle non-finite values.
Results may differ from a plain program's by a relative error of at most 0.017.
Values may be sent and summed in bfloat16 or wider, within the bound.
No kernel may reach another device: no remote copies, remote signals or barrier semaphores. Data moves between devices by JAX's collectives and lax.ppermute only.
A program may use at most 64 MiB of HBM per device.

v0:
```python
import jax
import jax.numpy as jnp
from jax import lax
from jax.sharding import PartitionSpec as P


def route_slots(block_ids, expert_count, capacity):
    flat_ids = block_ids.reshape(-1)
    onehot = (flat_ids[:, None] == jnp.arange(expert_count, dtype=jnp.int32)[None, :]).astype(
        jnp.int32
    )
    position = jnp.sum((jnp.cumsum(onehot, axis=0) - 1) * onehot, axis=1)
    return flat_ids * capacity + position


def expert_half(routed, grads_in, gate_vals, gate_cols, up_cols, down_cols):
    contract_last = (((1,), (1,)), ((), ()))
    gate_pre = jnp.dot(routed, gate_cols, preferred_element_type=jnp.float32)
    up_pre = jnp.dot(routed, up_cols, preferred_element_type=jnp.float32)
    sigmoid_val = jax.nn.sigmoid(gate_pre)
    activated = gate_pre * sigmoid_val
    hidden = (activated * up_pre).astype(jnp.bfloat16)
    produced = lax.dot_general(hidden, down_cols, contract_last, preferred_element_type=jnp.float32)
    gate_inner = jnp.sum(grads_in.astype(jnp.float32) * produced, axis=1)
    scaled = (gate_vals[:, None] * grads_in.astype(jnp.float32)).astype(jnp.bfloat16)
    hidden_grad = jnp.dot(scaled, down_cols, preferred_element_type=jnp.float32)
    gate_grad = (
        hidden_grad * up_pre * sigmoid_val * (1.0 + gate_pre * (1.0 - sigmoid_val))
    ).astype(jnp.bfloat16)
    up_grad = (hidden_grad * activated).astype(jnp.bfloat16)
    back_sum = lax.dot_general(
        gate_grad, gate_cols, contract_last, preferred_element_type=jnp.float32
    )
    back_sum = back_sum + lax.dot_general(
        up_grad, up_cols, contract_last, preferred_element_type=jnp.float32
    )
    return (hidden, scaled, gate_grad, up_grad, back_sum.astype(jnp.bfloat16), gate_inner)


def per_device(tokens, out_grad, expert_ids, gate_values, gate_weight, up_weight, down_weight):
    tok_count, model_width = tokens.shape
    expert_span = lax.axis_size("expert")
    seq_count = lax.axis_size("seq")
    expert_count = expert_span * gate_weight.shape[0]
    capacity = min(tok_count, 3 * tok_count // expert_span)
    half_width = gate_weight.shape[2]
    slot_index = route_slots(expert_ids, expert_count, capacity)
    pair_ids = jnp.arange(2 * tok_count, dtype=jnp.int32)
    sources = (
        jnp.full((expert_count * capacity,), 2 * tok_count, jnp.int32).at[slot_index].set(pair_ids)
    )
    token_source = sources // 2
    send_rows = jnp.take(tokens, token_source, axis=0, mode="fill", fill_value=0).reshape(
        expert_count, capacity, model_width
    )
    send_grads = jnp.take(out_grad, token_source, axis=0, mode="fill", fill_value=0).reshape(
        expert_count, capacity, model_width
    )
    send_gates = jnp.take(
        gate_values.reshape(-1), sources, axis=0, mode="fill", fill_value=0
    ).reshape(expert_count, capacity)
    full_gate, full_up, full_down = (
        lax.all_gather(gate_weight[0], "dp", axis=0, tiled=True),
        lax.all_gather(up_weight[0], "dp", axis=0, tiled=True),
        lax.all_gather(down_weight[0], "dp", axis=0, tiled=True),
    )

    def duplicate(source_array):
        widened = jnp.broadcast_to(
            source_array[:, None], (source_array.shape[0], seq_count) + source_array.shape[1:]
        )
        return widened.reshape((source_array.shape[0] * seq_count,) + source_array.shape[1:])

    got_rows, got_grads, got_gates = (
        lax.all_to_all(
            duplicate(send_rows), ("expert", "seq"), split_axis=0, concat_axis=0, tiled=True
        ),
        lax.all_to_all(
            duplicate(send_grads), ("expert", "seq"), split_axis=0, concat_axis=0, tiled=True
        ),
        lax.all_to_all(
            duplicate(send_gates).astype(jnp.bfloat16),
            ("expert", "seq"),
            split_axis=0,
            concat_axis=0,
            tiled=True,
        ).astype(jnp.float32),
    )
    routed_all = got_rows.reshape(-1, model_width)
    grads_all = got_grads.reshape(-1, model_width)
    gates_all = got_gates.reshape(-1)
    hidden, scaled, gate_grad, up_grad, back_grad, gate_inner = expert_half(
        routed_all, grads_all, gates_all, full_gate, full_up, full_down
    )
    contract_first = (((0,), (0,)), ((), ()))
    gate_term = lax.dot_general(
        routed_all, gate_grad, contract_first, preferred_element_type=jnp.float32
    )
    up_term = lax.dot_general(
        routed_all, up_grad, contract_first, preferred_element_type=jnp.float32
    )
    down_term = lax.dot_general(scaled, hidden, contract_first, preferred_element_type=jnp.float32)
    summed_grads = lax.psum_scatter(
        jnp.concatenate([gate_term, up_term, down_term], axis=1).astype(jnp.bfloat16),
        "dp",
        scatter_dimension=0,
        tiled=True,
    ).astype(jnp.float32)
    back_parts, inner_parts = (
        lax.all_to_all(
            back_grad.reshape(expert_count * seq_count, capacity, model_width),
            ("expert", "seq"),
            split_axis=0,
            concat_axis=0,
            tiled=True,
        ),
        lax.all_to_all(
            gate_inner.reshape(expert_count * seq_count, capacity).astype(jnp.bfloat16),
            ("expert", "seq"),
            split_axis=0,
            concat_axis=0,
            tiled=True,
        ).astype(jnp.float32),
    )
    back_parts = back_parts.reshape(expert_count, seq_count, capacity, model_width)
    slot_grad = jnp.sum(back_parts.astype(jnp.float32), axis=1).astype(jnp.bfloat16)
    slot_inner = jnp.sum(inner_parts.reshape(expert_count, seq_count, capacity), axis=1)
    picked = slot_grad.reshape(-1, model_width)[slot_index].reshape(tok_count, 2, model_width)
    in_grad = jnp.sum(picked.astype(jnp.float32), axis=1).astype(jnp.bfloat16)
    gate_grads = slot_inner.reshape(-1)[slot_index].reshape(tok_count, 2)
    gate_weight_grad = summed_grads[:, :half_width].astype(jnp.bfloat16)[None]
    up_weight_grad = summed_grads[:, half_width : 2 * half_width].astype(jnp.bfloat16)[None]
    down_weight_grad = summed_grads[:, 2 * half_width :].astype(jnp.bfloat16)[None]
    return (in_grad, gate_grads, gate_weight_grad, up_weight_grad, down_weight_grad)


def solution(mesh):
    return jax.shard_map(
        per_device,
        mesh=mesh,
        in_specs=(
            P(("dp", "expert", "seq"), None),
            P(("dp", "expert", "seq"), None),
            P(("dp", "expert", "seq"), None),
            P(("dp", "expert", "seq"), None),
            P("expert", "dp", "seq"),
            P("expert", "dp", "seq"),
            P("expert", "dp", "seq"),
        ),
        out_specs=(
            P(("dp", "expert", "seq"), None),
            P(("dp", "expert", "seq"), None),
            P("expert", "dp", "seq"),
            P("expert", "dp", "seq"),
            P("expert", "dp", "seq"),
        ),
        check_vma=False,
    )
```

profile of v0, /device:TPU:0, one launch (start us, length us, event | category | flops | bytes accessed | tf_op | source)
XLA Modules:
  0.0 231.6 jit_solution(122135648007683980)
XLA Ops:
  7.2 0.7 broadcast_multiply_fusion
  7.9 0.8 copy.39
  9.0 0.8 copy.43
  10.2 1.2 reduce-window.6
  11.9 1.4 scatter_custom_fusion
  13.3 2.7 %gather_fusion = bf16[384]{0:T(512)(128)(2,1)S(1)} fusion(bf16[256]{0:T(256)(128)(2,1)S(1)} %reshape.155, s32[1024]{0:T(1024)S(1)} %pad_clamp_fusion.2), kind=kCustom, calls=%fused_computation.2 | custom fusion | bytes 3072 | tf_op jit(solution)/shard_map/jit(_take)/gather | solution.py:59
  16.1 0.6 copy.44
  16.7 5.2 %all-to-all-start = ((bf16[8,1,96]{2,1,0:T(2,128)(2,1)}), bf16[8,1,96]{2,1,0:T(2,128)(2,1)S(1)}, u32[]{:S(2)}, u32[]{:S(2)}) async-start(bf16[8,1,96]{2,1,0:T(2,128)(2,1)} %copy.44), calls=%async_computation | async-start | bytes 8192 | tf_op jit(solution)/shard_map/all_to_all | solution.py:81
  22.0 3.1 %gather_fusion.4 = bf16[384,2048]{1,0:T(8,128)(2,1)} fusion(bf16[128,2048]{1,0:T(8,128)(2,1)S(1)} %copy-done, s32[1024]{0:T(1024)S(1)} %pad_clamp_fusion.1), kind=kCustom, calls=%fused_computation.1.clone | custom fusion | bytes 3147264 | tf_op jit(solution)/shard_map/jit(_take)/gather | solution.py:53
  25.1 3.1 %gather_fusion.3 = bf16[384,2048]{1,0:T(8,128)(2,1)} fusion(bf16[128,2048]{1,0:T(8,128)(2,1)S(1)} %copy-done.1, s32[1024]{0:T(1024)S(1)} %pad_clamp_fusion.1), kind=kCustom, calls=%fused_computation.clone | custom fusion | bytes 3147264 | tf_op jit(solution)/shard_map/jit(_take)/gather | solution.py:56
  28.2 3.3 %broadcast_select_fusion.1 = (bf16[384,2048]{1,0:T(8,128)(2,1)S(1)}, bf16[384,2048]{1,0:T(8,128)(2,1)}) fusion(bf16[384,2048]{1,0:T(8,128)(2,1)} %gather_fusion.3, pred[384]{0:T(512)(128)(4,1)S(1)} %get-tuple-element.26, bf16[384,2048]{1,0:T(8,128)(2,1)} %gather_fusion.4), kind=kLoop, calls=%fused_computation.17 | loop fusion | flops 1572864 | bytes 6291840 | tf_op jit(solution)/shard_map/jit(_take)/select_n | solution.py:56
  31.5 3.5 %broadcast_in_dim.59 = bf16[4,2,96,2048]{3,2,1,0:T(8,128)(2,1)} broadcast(bf16[4,96,2048]{2,1,0:T(8,128)(2,1)} %bitcast.72), dimensions={0,2,3} | broadcast | bytes 4718592 | tf_op jit(solution)/shard_map/broadcast_in_dim | solution.py:69
  35.0 4.4 %all-to-all-start.2 = ((bf16[8,96,2048]{2,1,0:T(8,128)(2,1)}), bf16[8,96,2048]{2,1,0:T(8,128)(2,1)}, u32[]{:S(2)}, u32[]{:S(2)}) async-start(bf16[8,96,2048]{2,1,0:T(8,128)(2,1)} %bitcast.69), calls=%async_computation.2 | async-start | bytes 6291456 | tf_op jit(solution)/shard_map/all_to_all | solution.py:75
  39.5 0.7 all-gather.11.cloned.1.call-update
  40.2 37.1 %all-to-all-done.2 = bf16[8,96,2048]{2,1,0:T(8,128)(2,1)} async-done(((bf16[8,96,2048]{2,1,0:T(8,128)(2,1)}), bf16[8,96,2048]{2,1,0:T(8,128)(2,1)}, u32[]{:S(2)}, u32[]{:S(2)}) %all-to-all-start.2) | async-done | bytes 3145760 | tf_op jit(solution)/shard_map/all_to_all | solution.py:75
  77.3 2.1 broadcast_in_dim.57
  79.4 4.4 %all-to-all-start.1 = ((bf16[8,96,2048]{2,1,0:T(8,128)(2,1)}), bf16[8,96,2048]{2,1,0:T(8,128)(2,1)}, u32[]{:S(2)}, u32[]{:S(2)}) async-start(bf16[8,96,2048]{2,1,0:T(8,128)(2,1)} %bitcast.68), calls=%async_computation.1 | async-start | bytes 6291456 | tf_op jit(solution)/shard_map/all_to_all | solution.py:78
  83.9 0.7 all-gather.7.cloned.1.call-update
  84.6 0.7 all-gather.9.cloned.1.call-update
  85.7 3.2 %fusion.4 = f32[768,256]{1,0:T(8,128)S(1)} fusion(bf16[768,2048]{1,0:T(8,128)(2,1)} %bitcast.11, bf16[1,2048,256]{2,1,0:T(8,128)(2,1)} %all-gather.11.cloned.1.call-done), kind=kOutput, calls=%fused_computation.20 | convolution fusion | flops 805306368 | bytes 4980736 | tf_op jit(solution)/shard_map/dot_general | solution.py:18
  88.8 32.9 %all-to-all-done.1 = bf16[8,96,2048]{2,1,0:T(8,128)(2,1)} async-done(((bf16[8,96,2048]{2,1,0:T(8,128)(2,1)}), bf16[8,96,2048]{2,1,0:T(8,128)(2,1)}, u32[]{:S(2)}, u32[]{:S(2)}) %all-to-all-start.1) | async-done | bytes 3145760 | tf_op jit(solution)/shard_map/all_to_all | solution.py:78
  121.7 4.2 %fusion = bf16[768,2048]{1,0:T(8,128)(2,1)} fusion(bf16[8,96,2048]{2,1,0:T(8,128)(2,1)} %all-to-all-done.1, f32[768]{0:T(1024)S(1)} %reshape.165), kind=kLoop, calls=%fused_computation.8 | loop fusion | flops 4718592 | bytes 6294528 | tf_op jit(solution)/shard_map/convert_element_type | solution.py:25
  125.9 3.2 %fusion.10 = f32[768,256]{1,0:T(8,128)S(1)} fusion(bf16[768,2048]{1,0:T(8,128)(2,1)} %fusion, bf16[1,2048,256]{2,1,0:T(8,128)(2,1)} %all-gather.7.cloned.1.call-done), kind=kOutput, calls=%fused_computation.26 | convolution fusion | flops 805306368 | bytes 4980736 | tf_op jit(solution)/shard_map/dot_general | solution.py:26
  129.1 15.8 %all-gather.9.cloned.1.call-done = bf16[1,2048,256]{2,1,0:T(8,128)(2,1)} async-done(((bf16[1,512,256]{2,1,0:T(8,128)(2,1)}), bf16[1,2048,256]{2,1,0:T(8,128)(2,1)}) %all-gather.9.cloned.1.call-update) | async-done | bytes 1048592 | tf_op jit(solution)/shard_map/all_gather | solution.py:64
  144.8 3.5 %multiply_convert_fusion = (bf16[768,256]{1,0:T(8,128)(2,1)S(1)}, bf16[768,256]{1,0:T(8,128)(2,1)S(1)}, bf16[768,256]{1,0:T(8,128)(2,1)S(1)}) fusion(f32[768,256]{1,0:T(8,128)S(1)} %fusion.4, f32[768,256]{1,0:T(8,128)S(1)} %fusion.10, bf16[768,2048]{1,0:T(8,128)(2,1)} %bitcast.11, bf16[1,2048,256]{2,1,0:T(8,128)(2,1)} %all-gather.9.cloned.1.call-done), kind=kOutput, calls=%fused_computation.28 | convolution fusion | flops 808255488 | bytes 6946816 | tf_op jit(solution)/shard_map/dot_general | solution.py:19
  148.4 1.0 convolution_convert_fusion
  149.5 2.9 %convolution_convert_fusion.2 = bf16[2048,256]{0,1:T(8,128)(2,1)S(1)} fusion(bf16[768,2048]{1,0:T(8,128)(2,1)} %bitcast.11, bf16[768,256]{1,0:T(8,128)(2,1)S(1)} %get-tuple-element.29), kind=kOutput, calls=%fused_computation.15 | convolution fusion | flops 805830656 | bytes 4587520 | tf_op jit(solution)/shard_map/dot_general | solution.py:96
  152.4 2.9 %convolution_convert_fusion.1 = bf16[2048,256]{0,1:T(8,128)(2,1)S(1)} fusion(bf16[768,2048]{1,0:T(8,128)(2,1)} %bitcast.11, bf16[768,256]{1,0:T(8,128)(2,1)S(1)} %get-tuple-element.30), kind=kOutput, calls=%fused_computation.14 | convolution fusion | flops 805830656 | bytes 4587520 | tf_op jit(solution)/shard_map/dot_general | solution.py:99
  155.3 1.9 pad_maximum_fusion
  157.2 1.2 copy-done.5
  158.4 3.2 %fusion.1 = bf16[768]{0:T(1024)(128)(2,1)S(1)} fusion(bf16[768,2048]{1,0:T(8,128)(2,1)} %bitcast.17, bf16[768,256]{1,0:T(8,128)(2,1)} %copy-done.6, bf16[1,2048,256]{2,1,0:T(8,128)(2,1)S(1)} %copy-done.5), kind=kOutput, calls=%fused_computation.9 | convolution fusion | flops 810024192 | bytes 4589056 | tf_op jit(solution)/shard_map/dot_general | solution.py:23
  161.6 0.7 convert_element_type.107
  162.3 3.7 %all-to-all-start.4 = ((bf16[8,1,96]{2,1,0:T(2,128)(2,1)}), bf16[8,1,96]{2,1,0:T(2,128)(2,1)S(1)}, u32[]{:S(2)}, u32[]{:S(2)}) async-start(bf16[8,1,96]{2,1,0:T(2,128)(2,1)} %convert_element_type.107), calls=%async_computation.4 | async-start | bytes 8192 | tf_op jit(solution)/shard_map/all_to_all | solution.py:117
  166.0 1.0 fusion.2
  167.2 2.8 %add_convert_fusion = bf16[768,2048]{1,0:T(8,128)(2,1)} fusion(f32[768,2048]{1,0:T(8,128)S(1)} %fusion.2, bf16[768,256]{1,0:T(8,128)(2,1)S(1)} %get-tuple-element.30, bf16[1,2048,256]{2,1,0:T(8,128)(2,1)S(1)} %copy-done.4), kind=kOutput, calls=%fused_computation.10 | convolution fusion | flops 808452096 | bytes 10878976 | tf_op jit(solution)/shard_map/dot_general | solution.py:34
  170.0 0.6 all-to-all-done.4
  170.6 4.7 %all-to-all-start.3 = ((bf16[8,96,2048]{2,1,0:T(8,128)(2,1)}), bf16[8,96,2048]{2,1,0:T(8,128)(2,1)}, u32[]{:S(2)}, u32[]{:S(2)}) async-start(bf16[8,96,2048]{2,1,0:T(8,128)(2,1)} %bitcast.70), calls=%async_computation.3 | async-start | bytes 6291456 | tf_op jit(solution)/shard_map/all_to_all | solution.py:110
  175.4 1.9 gather_fusion.2
  177.5 0.6 copy.46
  178.1 34.8 %all-to-all-done.3 = bf16[8,96,2048]{2,1,0:T(8,128)(2,1)} async-done(((bf16[8,96,2048]{2,1,0:T(8,128)(2,1)}), bf16[8,96,2048]{2,1,0:T(8,128)(2,1)}, u32[]{:S(2)}, u32[]{:S(2)}) %all-to-all-start.3) | async-done | bytes 3145760 | tf_op jit(solution)/shard_map/all_to_all | solution.py:110
  212.9 2.8 %bitcast_reduce_fusion = bf16[4,96,2048]{2,1,0:T(8,128)(2,1)S(1)} fusion(bf16[8,96,2048]{2,1,0:T(8,128)(2,1)} %all-to-all-done.3), kind=kLoop, calls=%fused_computation.12 | loop fusion | flops 786432 | bytes 4718592 | tf_op jit(solution)/shard_map/reduce_sum | solution.py:126
  215.6 1.4 gather_fusion.1
  217.0 0.7 reshape.162
  217.7 3.6 %reduce_sum.56 = bf16[128,2048]{1,0:T(8,128)(2,1)} reduce(bf16[128,2,2048]{2,1,0:T(2,128)(2,1)S(1)} %reshape.162, bf16[]{:T(256)} %constant.57.clone.1), dimensions={1}, to_apply=%region_5.7 | reduce | flops 262144 | bytes 1572866 | tf_op jit(solution)/shard_map/reduce_sum | solution.py:129
  221.4 1.2 slice_bitcast_fusion
  222.5 0.8 copy.49
  223.4 0.8 copy.48
  224.2 0.8 copy.47
  (51 shorter events, 2.2 us)
Async XLA Ops:
  7.2 14.8 %copy-start = (bf16[128,2048]{1,0:T(8,128)(2,1)S(1)}, bf16[128,2048]{1,0:T(8,128)(2,1)}, u32[]{:S(2)}) copy-start(bf16[128,2048]{1,0:T(8,128)(2,1)} %param.9) | copy-start | bytes 1572868
  16.7 14.8 %all-to-all-start = ((bf16[8,1,96]{2,1,0:T(2,128)(2,1)}), bf16[8,1,96]{2,1,0:T(2,128)(2,1)S(1)}, u32[]{:S(2)}, u32[]{:S(2)}) async-start(bf16[8,1,96]{2,1,0:T(2,128)(2,1)} %copy.44), calls=%async_computation | async-start | bytes 8192 | tf_op jit(solution)/shard_map/all_to_all | solution.py:81
  22.0 3.1 %copy-start.1 = (bf16[128,2048]{1,0:T(8,128)(2,1)S(1)}, bf16[128,2048]{1,0:T(8,128)(2,1)}, u32[]{:S(2)}) copy-start(bf16[128,2048]{1,0:T(8,128)(2,1)} %param.10) | copy-start | bytes 1572868
  35.0 42.3 %all-to-all-start.2 = ((bf16[8,96,2048]{2,1,0:T(8,128)(2,1)}), bf16[8,96,2048]{2,1,0:T(8,128)(2,1)}, u32[]{:S(2)}, u32[]{:S(2)}) async-start(bf16[8,96,2048]{2,1,0:T(8,128)(2,1)} %bitcast.69), calls=%async_computation.2 | async-start | bytes 6291456 | tf_op jit(solution)/shard_map/all_to_all | solution.py:75
  39.4 46.2 %all-gather.11.cloned.1.call-start = ((), (), s32[]{:S(2)}) async-start(), calls=%async_computation.9 | async-start | bytes 1310720 | tf_op jit(solution)/shard_map/all_gather | solution.py:63
  79.4 42.3 %all-to-all-start.1 = ((bf16[8,96,2048]{2,1,0:T(8,128)(2,1)}), bf16[8,96,2048]{2,1,0:T(8,128)(2,1)}, u32[]{:S(2)}, u32[]{:S(2)}) async-start(bf16[8,96,2048]{2,1,0:T(8,128)(2,1)} %bitcast.68), calls=%async_computation.1 | async-start | bytes 6291456 | tf_op jit(solution)/shard_map/all_to_all | solution.py:78
  83.8 42.1 %all-gather.7.cloned.1.call-start = ((), (), s32[]{:S(2)}) async-start(), calls=%async_computation.7 | async-start | bytes 1310720 | tf_op jit(solution)/shard_map/all_gather | solution.py:65
  84.6 60.2 %all-gather.9.cloned.1.call-start = ((), (), s32[]{:S(2)}) async-start(), calls=%async_computation.8 | async-start | bytes 1310720 | tf_op jit(solution)/shard_map/all_gather | solution.py:64
  85.3 136.0 %reduce-scatter.2.cloned.1.call-start = ((), (), s32[]{:S(2)}) async-start(), calls=%async_computation.6 | async-start | bytes 3932160 | tf_op jit(solution)/shard_map/reduce_scatter | solution.py:103
  144.8 3.6 %copy-start.2 = (bf16[768,2048]{1,0:T(8,128)(2,1)S(1)}, bf16[768,2048]{1,0:T(8,128)(2,1)}, u32[]{:S(2)}) copy-start(bf16[768,2048]{1,0:T(8,128)(2,1)} %fusion) | copy-start | bytes 9437188
  148.4 1.1 copy-start.6
  157.2 1.2 copy-start.5
  158.4 7.6 %copy-start.3 = (bf16[1,2048,256]{2,1,0:T(8,128)(2,1)S(1)}, bf16[1,2048,256]{2,1,0:T(8,128)(2,1)}, u32[]{:S(2)}) copy-start(bf16[1,2048,256]{2,1,0:T(8,128)(2,1)} %all-gather.11.cloned.1.call-done) | copy-start | bytes 3145732
  162.3 8.3 %all-to-all-start.4 = ((bf16[8,1,96]{2,1,0:T(2,128)(2,1)}), bf16[8,1,96]{2,1,0:T(2,128)(2,1)S(1)}, u32[]{:S(2)}, u32[]{:S(2)}) async-start(bf16[8,1,96]{2,1,0:T(2,128)(2,1)} %convert_element_type.107), calls=%async_computation.4 | async-start | bytes 8192 | tf_op jit(solution)/shard_map/all_to_all | solution.py:117
  166.0 1.2 copy-start.4
  170.6 42.3 %all-to-all-start.3 = ((bf16[8,96,2048]{2,1,0:T(8,128)(2,1)}), bf16[8,96,2048]{2,1,0:T(8,128)(2,1)}, u32[]{:S(2)}, u32[]{:S(2)}) async-start(bf16[8,96,2048]{2,1,0:T(8,128)(2,1)} %bitcast.70), calls=%async_computation.3 | async-start | bytes 6291456 | tf_op jit(solution)/shard_map/all_to_all | solution.py:110
Sparse Core Ops, SparseCore 0:
  41.8 29.6 all-gather.10
  86.2 29.5 all-gather.6
  117.4 27.3 all-gather.8
  157.3 59.8 reduce-scatter.1
where the time goes:
time: 232 us
  waiting for transfers between devices  123 us (53%)
  local copies, waits for them, and re-layouts  29.9 us (13%)
  matrix products  23.7 us (10%)
  starting transfers between devices  22.8 us (10%)
  other arithmetic  18 us (8%)
  between operations  14 us (6%)
    all_to_all x1, waiting for transfers between devices, per_device(): lax.all_to_all(duplicate(send_rows), ('expert', 'seq'), split_axis=0, con...  37.1 us
    all_to_all x1, waiting for transfers between devices, per_device(): lax.all_to_all(back_grad.reshape(expert_count * seq_count, capacity, mode...  34.8 us
    all_to_all x1, waiting for transfers between devices, per_device(): lax.all_to_all(duplicate(send_grads), ('expert', 'seq'), split_axis=0, co...  32.9 us
    all_gather x1, waiting for transfers between devices, per_device(): lax.all_gather(up_weight[0], 'dp', axis=0, tiled=True)  15.8 us
    unnamed x20, local copies, waits for them, and re-layouts  6.18 us
    broadcast_in_dim x3, local copies, waits for them, and re-layouts, duplicate(): jnp.broadcast_to(source_array[:, None], (source_array.shape[0], seq_count...  5.55 us
    all_to_all x1, starting transfers between devices, per_device(): lax.all_to_all(duplicate(send_gates).astype(jnp.bfloat16), ('expert', 'se...  5.2 us
    all_to_all x1, starting transfers between devices, per_device(): lax.all_to_all(back_grad.reshape(expert_count * seq_count, capacity, mode...  4.67 us
  transfers between devices with their start and end apart: 9, of which 5 were waited for; matrix products, arithmetic and copies ran while one was open for 18% of the time, Pallas kernels for 0%

commit v1 on v0

--- a/solution.py
+++ b/solution.py
@@ -2,6 +2,22 @@
 import jax.numpy as jnp
 from jax import lax
 from jax.sharding import PartitionSpec as P
+
+
+def pairwise_exchange(x, axis, split, join):
+    ways, here = (lax.axis_size(axis), lax.axis_index(axis))
+    width = x.shape[split] // ways
+    shape = list(x.shape)
+    shape[split] = width
+    height = shape[join]
+    shape[join] = height * ways
+    full = jnp.zeros(shape, x.dtype)
+    for mask in range(ways):
+        part = lax.dynamic_slice_in_dim(x, (here ^ mask) * width, width, axis=split)
+        if mask:
+            part = lax.ppermute(part, axis, [(d, d ^ mask) for d in range(ways)])
+        full = lax.dynamic_update_slice_in_dim(full, part, (here ^ mask) * height, axis=join)
+    return full
 
 
 def route_slots(block_ids, expert_count, capacity):
@@ -75,9 +91,7 @@
         lax.all_to_all(
             duplicate(send_rows), ("expert", "seq"), split_axis=0, concat_axis=0, tiled=True
         ),
-        lax.all_to_all(
-            duplicate(send_grads), ("expert", "seq"), split_axis=0, concat_axis=0, tiled=True
-        ),
+        pairwise_exchange(duplicate(send_grads), ("expert", "seq"), 0, 0),
         lax.all_to_all(
             duplicate(send_gates).astype(jnp.bfloat16),
             ("expert", "seq"),

time: 232 us -> 210 us (0.905)
  waiting for transfers between devices: 123 us -> 92 us
  local copies, waits for them, and re-layouts: 29.9 us -> 37 us
    ppermute x0 -> x7, waiting for transfers between devices: none -> 55.2 us  [pairwise_exchange(): part = lax.ppermute(part, axis, [(d, d ^ mask) for d in range(ways)])]
    all_to_all x1, waiting for transfers between devices: 37.1 us -> 0.01 us  [per_device(): lax.all_to_all(duplicate(send_rows), ('expert', 'seq'), split_axis=0, con...]
    all_to_all x1 -> x0, waiting for transfers between devices: 32.9 us -> none  [per_device(): lax.all_to_all(duplicate(send_grads), ('expert', 'seq'), split_axis=0, co...]
    all_gather x1, waiting for transfers between devices: 15.8 us -> 0.02 us  [per_device(): lax.all_gather(up_weight[0], 'dp', axis=0, tiled=True)]
    ppermute x0 -> x7, starting transfers between devices: none -> 6.65 us  [pairwise_exchange(): part = lax.ppermute(part, axis, [(d, d ^ mask) for d in range(ways)])]
    dynamic_update_slice x0 -> x7, local copies, waits for them, and re-layouts: none -> 5.61 us  [pairwise_exchange(): lax.dynamic_update_slice_in_dim(full, part, (here ^ mask) * height, axis=...]
    all_to_all x1 -> x0, starting transfers between devices: 4.44 us -> none  [per_device(): lax.all_to_all(duplicate(send_grads), ('expert', 'seq'), split_axis=0, co...]
    unnamed x20 -> x22, local copies, waits for them, and re-layouts: 6.18 us -> 7.66 us
  transfers between devices with their start and end apart: 9 -> 15, of which waited for: 5 -> 6; matrix products, arithmetic and copies ran while one was open for 18% -> 29% of each run, Pallas kernels for 0% -> 0%
where the time goes in v1:
time: 210 us; the launch traced here: 209 us
  waiting for transfers between devices  92 us (44%)
  local copies, waits for them, and re-layouts  37 us (18%)
  starting transfers between devices  24.6 us (12%)
  matrix products  23.9 us (11%)
  other arithmetic  17.8 us (8%)
  between operations  14.1 us (7%)
    ppermute x7, waiting for transfers between devices, pairwise_exchange(): part = lax.ppermute(part, axis, [(d, d ^ mask) for d in range(ways)])  55.2 us
    all_to_all x1, waiting for transfers between devices, per_device(): lax.all_to_all(back_grad.reshape(expert_count * seq_count, capacity, mode...  34.8 us
    unnamed x22, local copies, waits for them, and re-layouts  7.66 us
    ppermute x7, starting transfers between devices, pairwise_exchange(): part = lax.ppermute(part, axis, [(d, d ^ mask) for d in range(ways)])  6.65 us
    dynamic_update_slice x7, local copies, waits for them, and re-layouts, pairwise_exchange(): lax.dynamic_update_slice_in_dim(full, part, (here ^ mask) * height, axis=...  5.61 us
    all_to_all x1, starting transfers between devices, per_device(): lax.all_to_all(duplicate(send_gates).astype(jnp.bfloat16), ('expert', 'se...  5.2 us
    all_to_all x1, starting transfers between devices, per_device(): lax.all_to_all(back_grad.reshape(expert_count * seq_count, capacity, mode...  4.67 us
    all_to_all x1, starting transfers between devices, per_device(): lax.all_to_all(duplicate(send_rows), ('expert', 'seq'), split_axis=0, con...  4.44 us
  transfers between devices with their start and end apart: 15, of which 6 were waited for; matrix products, arithmetic and copies ran while one was open for 29% of the time, Pallas kernels for 0%

profile of v1, /device:TPU:0, one launch (start us, length us, event | category | flops | bytes accessed | tf_op | source)
XLA Modules:
  0.0 209.4 jit_solution(2579090520039520201)
XLA Ops:
  8.7 0.8 copy.39
  10.4 1.2 reduce-window.6
  12.3 1.4 scatter_custom_fusion
  13.8 0.8 copy.43
  14.7 2.7 %gather_fusion = bf16[384]{0:T(512)(128)(2,1)S(1)} fusion(bf16[256]{0:T(256)(128)(2,1)S(1)} %reshape.155, s32[1024]{0:T(1024)S(1)} %pad_clamp_fusion.2), kind=kCustom, calls=%fused_computation.2 | custom fusion | bytes 3072 | tf_op jit(solution)/shard_map/jit(_take)/gather | solution.py:75
  18.1 5.2 %all-to-all-start = ((bf16[8,1,96]{2,1,0:T(2,128)(2,1)}), bf16[8,1,96]{2,1,0:T(2,128)(2,1)S(1)}, u32[]{:S(2)}, u32[]{:S(2)}) async-start(bf16[8,1,96]{2,1,0:T(2,128)(2,1)} %copy.44), calls=%async_computation | async-start | bytes 8192 | tf_op jit(solution)/shard_map/all_to_all | solution.py:95
  23.4 3.1 %gather_fusion.3 = bf16[384,2048]{1,0:T(8,128)(2,1)} fusion(bf16[128,2048]{1,0:T(8,128)(2,1)S(1)} %copy-done, s32[1024]{0:T(1024)S(1)} %pad_clamp_fusion.1), kind=kCustom, calls=%fused_computation.clone | custom fusion | bytes 3147264 | tf_op jit(solution)/shard_map/jit(_take)/gather | solution.py:72
  26.5 3.1 %gather_fusion.4 = bf16[384,2048]{1,0:T(8,128)(2,1)} fusion(bf16[128,2048]{1,0:T(8,128)(2,1)S(1)} %copy-done.1, s32[1024]{0:T(1024)S(1)} %pad_clamp_fusion.1), kind=kCustom, calls=%fused_computation.1.clone | custom fusion | bytes 3147264 | tf_op jit(solution)/shard_map/jit(_take)/gather | solution.py:69
  29.6 3.3 %broadcast_select_fusion.1 = (bf16[384,2048]{1,0:T(8,128)(2,1)S(1)}, bf16[384,2048]{1,0:T(8,128)(2,1)}) fusion(bf16[384,2048]{1,0:T(8,128)(2,1)} %gather_fusion.3, pred[384]{0:T(512)(128)(4,1)S(1)} %get-tuple-element.26, bf16[384,2048]{1,0:T(8,128)(2,1)} %gather_fusion.4), kind=kLoop, calls=%fused_computation.17 | loop fusion | flops 1572864 | bytes 6291840 | tf_op jit(solution)/shard_map/jit(_take)/select_n | solution.py:72
  33.0 3.5 %broadcast_in_dim.63 = bf16[4,2,96,2048]{3,2,1,0:T(8,128)(2,1)} broadcast(bf16[4,96,2048]{2,1,0:T(8,128)(2,1)} %bitcast.72), dimensions={0,2,3} | broadcast | bytes 4718592 | tf_op jit(solution)/shard_map/broadcast_in_dim | solution.py:85
  36.5 4.4 %all-to-all-start.1 = ((bf16[8,96,2048]{2,1,0:T(8,128)(2,1)}), bf16[8,96,2048]{2,1,0:T(8,128)(2,1)}, u32[]{:S(2)}, u32[]{:S(2)}) async-start(bf16[8,96,2048]{2,1,0:T(8,128)(2,1)} %bitcast.67), calls=%async_computation.1 | async-start | bytes 6291456 | tf_op jit(solution)/shard_map/all_to_all | solution.py:91
  41.7 1.3 constant_dynamic-slice_fusion
  43.1 1.7 copy-done.2
  45.2 1.6 collective-permute-start.1
  46.9 1.7 collective-permute-start.3
  49.1 2.6 %collective-permute-start.5 = (bf16[1,96,2048]{2,1,0:T(8,128)(2,1)S(1)}, bf16[1,96,2048]{2,1,0:T(8,128)(2,1)S(1)}, u32[]{:S(2)}, u32[]{:S(2)}) collective-permute-start(bf16[1,96,2048]{2,1,0:T(8,128)(2,1)S(1)} %get-tuple-element.29), channel_id=1, source_target_pairs={{0,6},{1,7},{2,4},{3,5},{4,2},{5,3},{6,0},{7,1},{8,14},{9,15},{10,... | collective-permute-start | bytes 1179656 | tf_op jit(solution)/shard_map/ppermute | solution.py:18
  51.6 0.8 constant_dynamic-update-slice_fusion.5
  52.4 34.4 %collective-permute-done.1 = bf16[1,96,2048]{2,1,0:T(8,128)(2,1)S(1)} collective-permute-done((bf16[1,96,2048]{2,1,0:T(8,128)(2,1)}, bf16[1,96,2048]{2,1,0:T(8,128)(2,1)S(1)}, u32[]{:S(2)}, u32[]{:S(2)}) %collective-permute-start.1) | collective-permute-done | bytes 393248 | tf_op jit(solution)/shard_map/ppermute | solution.py:18
  87.7 6.4 %collective-permute-done.2 = bf16[1,96,2048]{2,1,0:T(8,128)(2,1)S(1)} collective-permute-done((bf16[1,96,2048]{2,1,0:T(8,128)(2,1)}, bf16[1,96,2048]{2,1,0:T(8,128)(2,1)S(1)}, u32[]{:S(2)}, u32[]{:S(2)}) %collective-permute-start.2) | collective-permute-done | bytes 393248 | tf_op jit(solution)/shard_map/ppermute | solution.py:18
  94.9 0.8 constant_dynamic-update-slice_fusion.2
  95.7 0.8 constant_dynamic-update-slice_fusion.1
  96.5 8.0 %collective-permute-done.5 = bf16[1,96,2048]{2,1,0:T(8,128)(2,1)S(1)} collective-permute-done((bf16[1,96,2048]{2,1,0:T(8,128)(2,1)S(1)}, bf16[1,96,2048]{2,1,0:T(8,128)(2,1)S(1)}, u32[]{:S(2)}, u32[]{:S(2)}) %collective-permute-start.5) | collective-permute-done | bytes 393248 | tf_op jit(solution)/shard_map/ppermute | solution.py:18
  104.6 0.8 constant_dynamic-update-slice_fusion
  105.4 6.5 %collective-permute-done.6 = bf16[1,96,2048]{2,1,0:T(8,128)(2,1)S(1)} collective-permute-done((bf16[1,96,2048]{2,1,0:T(8,128)(2,1)S(1)}, bf16[1,96,2048]{2,1,0:T(8,128)(2,1)S(1)}, u32[]{:S(2)}, u32[]{:S(2)}) %collective-permute-start.6) | collective-permute-done | bytes 393248 | tf_op jit(solution)/shard_map/ppermute | solution.py:18
  111.8 0.8 constant_dynamic-update-slice_fusion.6
  112.7 4.1 %fusion = bf16[768,2048]{1,0:T(8,128)(2,1)} fusion(bf16[8,96,2048]{2,1,0:T(8,128)(2,1)} %constant_dynamic-update-slice_fusion.6, f32[768]{0:T(1024)S(1)} %reshape.165), kind=kLoop, calls=%fused_computation.8 | loop fusion | flops 4718592 | bytes 6294528 | tf_op jit(solution)/shard_map/convert_element_type | solution.py:41
  116.8 3.2 %fusion.4 = f32[768,256]{1,0:T(8,128)S(1)} fusion(bf16[768,2048]{1,0:T(8,128)(2,1)} %bitcast.11, bf16[1,2048,256]{2,1,0:T(8,128)(2,1)} %all-gather.11.cloned.1.call-done), kind=kOutput, calls=%fused_computation.20 | convolution fusion | flops 805306368 | bytes 4980736 | tf_op jit(solution)/shard_map/dot_general | solution.py:34
  120.0 3.2 %fusion.7 = f32[768,256]{1,0:T(8,128)S(1)} fusion(bf16[768,2048]{1,0:T(8,128)(2,1)} %bitcast.11, bf16[1,2048,256]{2,1,0:T(8,128)(2,1)} %all-gather.9.cloned.1.call-done), kind=kOutput, calls=%fused_computation.23 | convolution fusion | flops 805306368 | bytes 4980736 | tf_op jit(solution)/shard_map/dot_general | solution.py:35
  123.2 3.5 %multiply_convert_fusion = (bf16[768,256]{1,0:T(8,128)(2,1)S(1)}, bf16[768,256]{1,0:T(8,128)(2,1)S(1)}, bf16[768,256]{1,0:T(8,128)(2,1)S(1)}) fusion(f32[768,256]{1,0:T(8,128)S(1)} %fusion.7, f32[768,256]{1,0:T(8,128)S(1)} %fusion.4, bf16[768,2048]{1,0:T(8,128)(2,1)} %fusion, bf16[1,2048,256]{2,1,0:T(8,128)(2,1)} %all-gather.7.cloned.1.call-done), kind=kOutput, calls=%fused_computation.28 | convolution fusion | flops 808255488 | bytes 6946816 | tf_op jit(solution)/shard_map/dot_general | solution.py:42
  126.7 1.0 convolution_convert_fusion
  127.8 2.9 %convolution_convert_fusion.1 = bf16[2048,256]{0,1:T(8,128)(2,1)S(1)} fusion(bf16[768,2048]{1,0:T(8,128)(2,1)} %bitcast.11, bf16[768,256]{1,0:T(8,128)(2,1)S(1)} %get-tuple-element.38), kind=kOutput, calls=%fused_computation.14 | convolution fusion | flops 805830656 | bytes 4587520 | tf_op jit(solution)/shard_map/dot_general | solution.py:113
  130.7 2.9 %convolution_convert_fusion.2 = bf16[2048,256]{0,1:T(8,128)(2,1)S(1)} fusion(bf16[768,2048]{1,0:T(8,128)(2,1)} %bitcast.11, bf16[768,256]{1,0:T(8,128)(2,1)S(1)} %get-tuple-element.37), kind=kOutput, calls=%fused_computation.15 | convolution fusion | flops 805830656 | bytes 4587520 | tf_op jit(solution)/shard_map/dot_general | solution.py:110
  133.6 1.8 pad_maximum_fusion
  135.4 1.0 copy-done.7
  136.4 3.4 %fusion.1 = bf16[768]{0:T(1024)(128)(2,1)S(1)} fusion(bf16[768,2048]{1,0:T(8,128)(2,1)} %bitcast.70, bf16[768,256]{1,0:T(8,128)(2,1)S(1)} %copy-done.7, bf16[1,2048,256]{2,1,0:T(8,128)(2,1)} %all-gather.7.cloned.1.call-done), kind=kOutput, calls=%fused_computation.9 | convolution fusion | flops 810024192 | bytes 4589056 | tf_op jit(solution)/shard_map/dot_general | solution.py:39
  140.5 3.3 %all-to-all-start.3 = ((bf16[8,1,96]{2,1,0:T(2,128)(2,1)}), bf16[8,1,96]{2,1,0:T(2,128)(2,1)S(1)}, u32[]{:S(2)}, u32[]{:S(2)}) async-start(bf16[8,1,96]{2,1,0:T(2,128)(2,1)} %convert_element_type.107), calls=%async_computation.3 | async-start | bytes 8192 | tf_op jit(solution)/shard_map/all_to_all | solution.py:131
  143.8 1.0 fusion.2
  145.0 2.8 %add_convert_fusion = bf16[768,2048]{1,0:T(8,128)(2,1)} fusion(f32[768,2048]{1,0:T(8,128)S(1)} %fusion.2, bf16[768,256]{1,0:T(8,128)(2,1)S(1)} %get-tuple-element.38, bf16[1,2048,256]{2,1,0:T(8,128)(2,1)S(1)} %copy-done.5), kind=kOutput, calls=%fused_computation.10 | convolution fusion | flops 808452096 | bytes 10878976 | tf_op jit(solution)/shard_map/dot_general | solution.py:50
  148.3 4.7 %all-to-all-start.2 = ((bf16[8,96,2048]{2,1,0:T(8,128)(2,1)}), bf16[8,96,2048]{2,1,0:T(8,128)(2,1)}, u32[]{:S(2)}, u32[]{:S(2)}) async-start(bf16[8,96,2048]{2,1,0:T(8,128)(2,1)} %bitcast.68), calls=%async_computation.2 | async-start | bytes 6291456 | tf_op jit(solution)/shard_map/all_to_all | solution.py:124
  153.2 1.9 gather_fusion.2
  155.9 34.8 %all-to-all-done.2 = bf16[8,96,2048]{2,1,0:T(8,128)(2,1)} async-done(((bf16[8,96,2048]{2,1,0:T(8,128)(2,1)}), bf16[8,96,2048]{2,1,0:T(8,128)(2,1)}, u32[]{:S(2)}, u32[]{:S(2)}) %all-to-all-start.2) | async-done | bytes 3145760 | tf_op jit(solution)/shard_map/all_to_all | solution.py:124
  190.7 2.8 %bitcast_reduce_fusion = bf16[4,96,2048]{2,1,0:T(8,128)(2,1)S(1)} fusion(bf16[8,96,2048]{2,1,0:T(8,128)(2,1)} %all-to-all-done.2), kind=kLoop, calls=%fused_computation.12 | loop fusion | flops 786432 | bytes 4718592 | tf_op jit(solution)/shard_map/reduce_sum | solution.py:140
  193.5 1.4 gather_fusion.1
  195.6 3.6 %reduce_sum.56 = bf16[128,2048]{1,0:T(8,128)(2,1)} reduce(bf16[128,2,2048]{2,1,0:T(2,128)(2,1)S(1)} %reshape.162, bf16[]{:T(256)} %constant.43.clone.1), dimensions={1}, to_apply=%region_5.7 | reduce | flops 262144 | bytes 1572866 | tf_op jit(solution)/shard_map/reduce_sum | solution.py:143
  199.2 1.2 slice_bitcast_fusion
  200.4 0.8 copy.47
  201.2 0.8 copy.48
  202.0 0.8 copy.49
  (74 shorter events, 10.5 us)
Async XLA Ops:
  7.2 16.2 %copy-start = (bf16[128,2048]{1,0:T(8,128)(2,1)S(1)}, bf16[128,2048]{1,0:T(8,128)(2,1)}, u32[]{:S(2)}) copy-start(bf16[128,2048]{1,0:T(8,128)(2,1)} %param.10) | copy-start | bytes 1572868
  7.2 109.6 %all-gather.11.cloned.1.call-start = ((), (), s32[]{:S(2)}) async-start(), calls=%async_computation.8 | async-start | bytes 1310720 | tf_op jit(solution)/shard_map/all_gather | solution.py:79
  7.9 112.0 %all-gather.9.cloned.1.call-start = ((), (), s32[]{:S(2)}) async-start(), calls=%async_computation.7 | async-start | bytes 1310720 | tf_op jit(solution)/shard_map/all_gather | solution.py:80
  18.1 14.8 %all-to-all-start = ((bf16[8,1,96]{2,1,0:T(2,128)(2,1)}), bf16[8,1,96]{2,1,0:T(2,128)(2,1)S(1)}, u32[]{:S(2)}, u32[]{:S(2)}) async-start(bf16[8,1,96]{2,1,0:T(2,128)(2,1)} %copy.44), calls=%async_computation | async-start | bytes 8192 | tf_op jit(solution)/shard_map/all_to_all | solution.py:95
  23.4 3.1 %copy-start.1 = (bf16[128,2048]{1,0:T(8,128)(2,1)S(1)}, bf16[128,2048]{1,0:T(8,128)(2,1)}, u32[]{:S(2)}) copy-start(bf16[128,2048]{1,0:T(8,128)(2,1)} %param.9) | copy-start | bytes 1572868
  36.5 80.3 %all-to-all-start.1 = ((bf16[8,96,2048]{2,1,0:T(8,128)(2,1)}), bf16[8,96,2048]{2,1,0:T(8,128)(2,1)}, u32[]{:S(2)}, u32[]{:S(2)}) async-start(bf16[8,96,2048]{2,1,0:T(8,128)(2,1)} %bitcast.67), calls=%async_computation.1 | async-start | bytes 6291456 | tf_op jit(solution)/shard_map/all_to_all | solution.py:91
  40.9 82.2 %all-gather.7.cloned.1.call-start = ((), (), s32[]{:S(2)}) async-start(), calls=%async_computation.6 | async-start | bytes 1310720 | tf_op jit(solution)/shard_map/all_gather | solution.py:81
  43.1 1.7 copy-start.2
  44.8 4.3 %collective-permute-start = (bf16[1,96,2048]{2,1,0:T(8,128)(2,1)}, bf16[1,96,2048]{2,1,0:T(8,128)(2,1)S(1)}, u32[]{:S(2)}, u32[]{:S(2)}) collective-permute-start(bf16[1,96,2048]{2,1,0:T(8,128)(2,1)} %get-tuple-element.34), channel_id=1, source_target_pairs={{0,1},{1,0},{2,3},{3,2},{4,5},{5,4},{6,7},{7,6},{8,9},{9,8},{10,11... | collective-permute-start | bytes 1179656 | tf_op jit(solution)/shard_map/ppermute | solution.py:18
  45.2 41.5 %collective-permute-start.1 = (bf16[1,96,2048]{2,1,0:T(8,128)(2,1)}, bf16[1,96,2048]{2,1,0:T(8,128)(2,1)S(1)}, u32[]{:S(2)}, u32[]{:S(2)}) collective-permute-start(bf16[1,96,2048]{2,1,0:T(8,128)(2,1)} %get-tuple-element.33), channel_id=1, source_target_pairs={{0,2},{1,3},{2,0},{3,1},{4,6},{5,7},{6,4},{7,5},{8,10},{9,11},{10,... | collective-permute-start | bytes 1179656 | tf_op jit(solution)/shard_map/ppermute | solution.py:18
  46.9 47.2 %collective-permute-start.2 = (bf16[1,96,2048]{2,1,0:T(8,128)(2,1)}, bf16[1,96,2048]{2,1,0:T(8,128)(2,1)S(1)}, u32[]{:S(2)}, u32[]{:S(2)}) collective-permute-start(bf16[1,96,2048]{2,1,0:T(8,128)(2,1)} %get-tuple-element.32), channel_id=1, source_target_pairs={{0,3},{1,2},{2,1},{3,0},{4,7},{5,6},{6,5},{7,4},{8,11},{9,10},{10,... | collective-permute-start | bytes 1179656 | tf_op jit(solution)/shard_map/ppermute | solution.py:18
  46.9 48.0 %collective-permute-start.3 = (bf16[1,96,2048]{2,1,0:T(8,128)(2,1)}, bf16[1,96,2048]{2,1,0:T(8,128)(2,1)S(1)}, u32[]{:S(2)}, u32[]{:S(2)}) collective-permute-start(bf16[1,96,2048]{2,1,0:T(8,128)(2,1)} %get-tuple-element.31), channel_id=1, source_target_pairs={{0,4},{1,5},{2,6},{3,7},{4,0},{5,1},{6,2},{7,3},{8,12},{9,13},{10,... | collective-permute-start | bytes 1179656 | tf_op jit(solution)/shard_map/ppermute | solution.py:18
  48.6 47.1 %collective-permute-start.4 = (bf16[1,96,2048]{2,1,0:T(8,128)(2,1)}, bf16[1,96,2048]{2,1,0:T(8,128)(2,1)S(1)}, u32[]{:S(2)}, u32[]{:S(2)}) collective-permute-start(bf16[1,96,2048]{2,1,0:T(8,128)(2,1)} %get-tuple-element.30), channel_id=1, source_target_pairs={{0,5},{1,4},{2,7},{3,6},{4,1},{5,0},{6,3},{7,2},{8,13},{9,12},{10,... | collective-permute-start | bytes 1179656 | tf_op jit(solution)/shard_map/ppermute | solution.py:18
  48.7 150.4 %reduce-scatter.2.cloned.1.call-start = ((), (), s32[]{:S(2)}) async-start(), calls=%async_computation.5 | async-start | bytes 3932160 | tf_op jit(solution)/shard_map/reduce_scatter | solution.py:117
  49.1 55.5 %collective-permute-start.5 = (bf16[1,96,2048]{2,1,0:T(8,128)(2,1)S(1)}, bf16[1,96,2048]{2,1,0:T(8,128)(2,1)S(1)}, u32[]{:S(2)}, u32[]{:S(2)}) collective-permute-start(bf16[1,96,2048]{2,1,0:T(8,128)(2,1)S(1)} %get-tuple-element.29), channel_id=1, source_target_pairs={{0,6},{1,7},{2,4},{3,5},{4,2},{5,3},{6,0},{7,1},{8,14},{9,15},{10,... | collective-permute-start | bytes 1179656 | tf_op jit(solution)/shard_map/ppermute | solution.py:18
  86.8 25.1 %collective-permute-start.6 = (bf16[1,96,2048]{2,1,0:T(8,128)(2,1)S(1)}, bf16[1,96,2048]{2,1,0:T(8,128)(2,1)S(1)}, u32[]{:S(2)}, u32[]{:S(2)}) collective-permute-start(bf16[1,96,2048]{2,1,0:T(8,128)(2,1)S(1)} %get-tuple-element.28), channel_id=1, source_target_pairs={{0,7},{1,6},{2,5},{3,4},{4,3},{5,2},{6,1},{7,0},{8,15},{9,14},{10,... | collective-permute-start | bytes 1179656 | tf_op jit(solution)/shard_map/ppermute | solution.py:18
  123.1 3.5 %copy-start.3 = (bf16[768,2048]{1,0:T(8,128)(2,1)S(1)}, bf16[768,2048]{1,0:T(8,128)(2,1)}, u32[]{:S(2)}) copy-start(bf16[768,2048]{1,0:T(8,128)(2,1)} %fusion) | copy-start | bytes 9437188
  126.7 1.1 copy-start.6
  135.4 1.0 copy-start.7
  136.4 7.4 %copy-start.4 = (bf16[1,2048,256]{2,1,0:T(8,128)(2,1)S(1)}, bf16[1,2048,256]{2,1,0:T(8,128)(2,1)}, u32[]{:S(2)}) copy-start(bf16[1,2048,256]{2,1,0:T(8,128)(2,1)} %all-gather.11.cloned.1.call-done) | copy-start | bytes 3145732
  140.5 7.9 %all-to-all-start.3 = ((bf16[8,1,96]{2,1,0:T(2,128)(2,1)}), bf16[8,1,96]{2,1,0:T(2,128)(2,1)S(1)}, u32[]{:S(2)}, u32[]{:S(2)}) async-start(bf16[8,1,96]{2,1,0:T(2,128)(2,1)} %convert_element_type.107), calls=%async_computation.3 | async-start | bytes 8192 | tf_op jit(solution)/shard_map/all_to_all | solution.py:131
  143.8 1.2 copy-start.5
  148.3 42.3 %all-to-all-start.2 = ((bf16[8,96,2048]{2,1,0:T(8,128)(2,1)}), bf16[8,96,2048]{2,1,0:T(8,128)(2,1)}, u32[]{:S(2)}, u32[]{:S(2)}) async-start(bf16[8,96,2048]{2,1,0:T(8,128)(2,1)} %bitcast.68), calls=%async_computation.2 | async-start | bytes 6291456 | tf_op jit(solution)/shard_map/all_to_all | solution.py:124
Sparse Core Ops, SparseCore 0:
  9.6 30.6 all-gather.10
  41.9 27.3 all-gather.8
  70.8 27.3 all-gather.6
  135.5 59.9 reduce-scatter.1
